TPU v7x, 32 devices: a whole 2x2x4 slice. The times are simulated.
32 devices in a mesh: orb: 4 (over y, x), grid: 8 (over z, core).
Axes of the slice: x: 2, y: 2, z: 4, core: 2. Of those that a mesh axis runs over, the one named last changes fastest.
Arguments:
- orbitals: float32 [4, 96, 192, 256], P('orb', 'grid'), may hold values from -6 to 6
- potential: float32 [96, 192, 256], P('grid'), may hold values from -4 to 0
- trial_potential: float32 [96, 192, 256], P('grid'), may hold values from -6 to 6
- eigenvalues: float32 [4], P('orb'), may hold values from -3 to 0
- frequency: float32 [1], replicated, may hold values from 1 to 8
Outputs:
- solutions: float32 [4, 96, 192, 256], P('orb', 'grid')
- density: float32 [96, 192, 256], P('grid', 'orb')
All inputs are finite; a program needn't handle non-finite values.
Results may differ from a plain program's by a relative error of at most 0.0001.
Values sent between devices are 32-bit elements; how exact they have to be, the bound alone decides.
A program may use at most 192 MiB of HBM per device.

v0:
```python
import functools

import jax
import jax.numpy as jnp
from jax import lax
from jax.experimental import pallas as pl
from jax.experimental.pallas import tpu as pltpu
from jax.sharding import PartitionSpec as P

STENCIL = (
    -5369.0 / 1800.0,
    12.0 / 7.0,
    -15.0 / 56.0,
    10.0 / 189.0,
    -1.0 / 112.0,
    2.0 / 1925.0,
    -1.0 / 16632.0,
)
SPACING = 0.75
REACH = len(STENCIL) - 1
COEFS = tuple(-0.5 / (SPACING * SPACING) * c for c in STENCIL)
STRIP = 8


def circulant(ref, count):
    size = ref.shape[1]

    def step(s, carry):
        rows = pl.ds(pl.multiple_of(s * count, count), count)
        row = s * count + lax.broadcasted_iota(jnp.int32, (count, size), 0)
        apart = jnp.abs(row - lax.broadcasted_iota(jnp.int32, (count, size), 1))
        apart = jnp.minimum(apart, size - apart)
        full = jnp.zeros((count, size), jnp.float32)
        for k in range(1, REACH + 1):
            full = jnp.where(apart == k, COEFS[k], full)
        high = full.astype(jnp.bfloat16)
        ref[0, rows, :] = high
        ref[1, rows, :] = (full - high.astype(jnp.float32)).astype(jnp.bfloat16)
        return carry

    lax.fori_loop(0, size // count, step, 0)


def kernel(
    n,
    orb_hbm, pot_hbm, tri_hbm, eig_hbm, freq_hbm,
    src, dens,
    orb, pot, tri, img, two, res, dirn, fin, cz, cy,
    hup, hlo, sums, coef, part, got, last, ship, land, mix,
    eig, freq, wave_up, wave_down, ld_sem, mat_sem,
    dn_s, dn_r, up_s, up_r, sum_s, sum_r, part_s, part_r, last_s, last_r,
    ship_s, ship_r, mix_s, mix_r,
):
    planes, ny, nz = src.shape
    wide = coef.shape[1]
    quarter = part.shape[2]
    g = lax.axis_index("grid")
    o = lax.axis_index("orb")
    below, above = lax.rem(g + n - 1, n), lax.rem(g + 1, n)
    has_low, has_up = g > 0, g < n - 1
    odd = lax.rem(g, 2)
    flip1 = o + 1 - 2 * lax.rem(o, 2)
    flip2 = lax.rem(o + 2, 4)
    first = (1 - odd) * flip1 + odd * flip2
    second = odd * flip1 + (1 - odd) * flip2
    both = 3 - o

    barrier = pltpu.get_barrier_semaphore()
    @pl.when(has_low)
    def _():
        pl.semaphore_signal(barrier, inc=1, device_id={"grid": below})

    @pl.when(has_up)
    def _():
        pl.semaphore_signal(barrier, inc=1, device_id={"grid": above})

    pl.semaphore_signal(barrier, inc=1, device_id={"orb": first})
    pl.semaphore_signal(barrier, inc=1, device_id={"orb": second})
    pl.semaphore_signal(barrier, inc=1, device_id={"orb": both})

    order = []
    for k in range(REACH):
        order += [k, planes - 1 - k]
    order += list(range(REACH, planes - REACH))

    def load(which, p):
        hbm, ref = ((orb_hbm, orb), (tri_hbm, tri))[which]
        return pltpu.make_async_copy(hbm.at[p], ref.at[p], ld_sem.at[which, p])

    for p in order:
        load(0, p).start()
        load(1, p).start()
    mats = [
        pltpu.make_async_copy(pot_hbm, pot, mat_sem.at[0]),
        pltpu.make_async_copy(eig_hbm, eig, mat_sem.at[1]),
        pltpu.make_async_copy(freq_hbm, freq, mat_sem.at[2]),
    ]
    for copy in mats:
        copy.start()

    fields = (src, img, res)

    def down(r, k):
        return pltpu.make_async_remote_copy(
            src_ref=fields[r].at[k], dst_ref=hup.at[r, k],
            send_sem=dn_s.at[r, k], recv_sem=dn_r.at[r, k],
            device_id={"grid": below}, device_id_type=pl.DeviceIdType.MESH)

    def up(r, k):
        return pltpu.make_async_remote_copy(
            src_ref=fields[r].at[planes - 1 - k], dst_ref=hlo.at[r, k],
            send_sem=up_s.at[r, k], recv_sem=up_r.at[r, k],
            device_id={"grid": above}, device_id_type=pl.DeviceIdType.MESH)

    def send(r, p):
        if p < REACH:
            @pl.when(has_low)
            def _():
                down(r, p).start()
        if p >= planes - REACH:
            @pl.when(has_up)
            def _():
                up(r, planes - 1 - p).start()

    edge = planes // 6
    middle = range(edge, planes - edge)
    outer = list(range(edge)) + list(range(planes - edge, planes))
    quarters = (both, first, second, o)

    def rows_in(slot):
        return pl.ds(pl.multiple_of(quarters[slot] * quarter, 8), quarter)

    def ship_copy(field, slot, p):
        return pltpu.make_async_remote_copy(
            src_ref=ship.at[field, slot, p - edge], dst_ref=land.at[field, slot, p - edge],
            send_sem=ship_s.at[field, slot, p - edge], recv_sem=ship_r.at[field, slot, p - edge],
            device_id={"orb": quarters[slot]}, device_id_type=pl.DeviceIdType.MESH)

    def share(field, value, p):
        if p in middle:
            for slot in range(3):
                rows = rows_in(slot)
                ship[field, slot, p - edge] = orb[p, rows, :] * value[p, rows, :]
                ship_copy(field, slot, p).start()

    def rows_of(s, count):
        return pl.ds(pl.multiple_of(s * count, count), count)

    def over(step, init, count=wide):
        return lax.fori_loop(0, ny // count, step, init)

    zero = jnp.zeros((wide, nz), jnp.float32)

    def upper_pairs(k):
        return [(p, COEFS[planes + k - p]) for p in range(planes - REACH + k, planes)]

    def lower_pairs(k):
        return [(p, COEFS[p + 1 + k]) for p in range(0, REACH - k)]

    def add_halo(acc, halo, pairs):
        def step(s, carry):
            rows = rows_of(s, wide)
            value = halo[rows, :]
            for p, c in pairs:
                acc[p, rows, :] = acc[p, rows, :] + c * value
            return carry

        over(step, 0)

    def arrive(r, k, acc, upper=None, lower=None):
        @pl.when(has_up)
        def _():
            down(r, k).wait_recv()
            add_halo(acc, hup.at[r, k], upper_pairs(k))

        @pl.when(has_low)
        def _():
            up(r, k).wait_recv()
            add_halo(acc, hlo.at[r, k], lower_pairs(k))

    def square_of(ref, p, total):
        def step(s, carry):
            value = ref[p, rows_of(s, wide), :]
            return carry + value * value

        return over(step, total)

    def interior(value, out):
        def plane(p, carry):
            whole = value[p]
            high = whole.astype(jnp.bfloat16)
            low = (whole - high.astype(jnp.float32)).astype(jnp.bfloat16)
            product = functools.partial(jnp.dot, preferred_element_type=jnp.float32)
            along_z = product(high, cz[0]) + product(low, cz[0]) + product(high, cz[1])
            along_y = product(cy[0], high) + product(cy[0], low) + product(cy[1], high)
            out[p] = along_z + along_y
            return carry

        lax.fori_loop(0, planes, plane, 0)

        def strip(s, carry):
            rows = rows_of(s, STRIP)
            parts = [value[q, rows, :] for q in range(planes)]
            for p in range(planes):
                total = out[p, rows, :] + (pot[p, rows, :] + (3.0 * COEFS[0] - energy)) * parts[p]
                for k in range(1, REACH + 1):
                    near = [parts[q] for q in (p - k, p + k) if 0 <= q < planes]
                    if near:
                        total = total + COEFS[k] * (near[0] + near[1] if len(near) == 2 else near[0])
                out[p, rows, :] = total
            return carry

        over(strip, 0, STRIP)

    def fold(total):
        total = functools.reduce(
            lambda a, b: a + b, [total[i:i + 8] for i in range(0, wide, 8)])
        return functools.reduce(
            lambda a, b: a + b, [total[:, i:i + 128] for i in range(0, nz, 128)])

    def exchange(r, j, slot):
        return pltpu.make_async_remote_copy(
            src_ref=sums.at[r, slot], dst_ref=sums.at[r, slot],
            send_sem=sum_s.at[r, j], recv_sem=sum_r.at[r, j],
            device_id={"grid": lax.rem(g + j, n)}, device_id_type=pl.DeviceIdType.MESH)

    def post(r, *totals):
        for i, total in enumerate(totals):
            sums[r, g, i] = fold(total)
        if len(totals) == 1:
            sums[r, g, 1] = jnp.zeros(sums.shape[3:], jnp.float32)
        for j in range(1, n):
            exchange(r, j, g).start()

    def collect(r, i):
        total = sums[r, 0, i]
        for m in range(1, n):
            total = total + sums[r, m, i]
        return jnp.sum(total, keepdims=True)

    def await_sums(r):
        for j in range(1, n):
            exchange(r, j, lax.rem(g + n - j, n)).wait_recv()

    def keep(i, value):
        coef[i] = jnp.broadcast_to(value, (wide, nz))

    pl.semaphore_wait(barrier, 3 + jnp.minimum(g, 1) + jnp.minimum(n - 1 - g, 1))
    total_src = zero
    for p in order:
        load(0, p).wait()
        load(1, p).wait()

        def step(s, carry, p=p):
            rows = rows_of(s, wide)
            value = orb[p, rows, :] * tri[p, rows, :]
            src[p, rows, :] = value
            return carry + value * value

        total_src = over(step, total_src)
        send(0, p)
    for copy in mats:
        copy.wait()
    energy = eig[0]
    squared = freq[0] * freq[0]

    circulant(cz, 32)
    circulant(cy, 32)
    def pass_on(wave, has_from, has_to, to):
        @pl.when(has_from)
        def _():
            pl.semaphore_wait(wave, 1)

        @pl.when(has_to)
        def _():
            pl.semaphore_signal(wave, inc=1, device_id={"grid": to})

    interior(src, img)
    pass_on(wave_up, has_low, has_up, above)
    pass_on(wave_down, has_up, has_low, below)

    total_img = zero
    for p in range(REACH, planes - REACH):
        total_img = square_of(img, p, total_img)
    held = []
    for k in range(REACH):
        arrive(0, k, img)
        for p in (REACH - 1 - k, planes - REACH + k):
            total_img = square_of(img, p, total_img)
            if k < REACH // 2:
                send(1, p)
            else:
                held.append(p)
    post(0, total_src, total_img)
    for p in held:
        send(1, p)
    for p in middle:
        share(0, img, p)

    interior(img, two)
    for k in range(REACH - 1, 0, -1):
        arrive(1, k, two)
    await_sums(0)
    norm0 = collect(0, 0)
    step0 = norm0 / (collect(0, 1) + squared * norm0)
    keep(0, step0)
    @pl.when(has_up)
    def _():
        down(1, 0).wait_recv()

    @pl.when(has_low)
    def _():
        up(1, 0).wait_recv()

    total_res = zero
    for p in order:
        if p < REACH:
            @pl.when(has_low)
            def _():
                add_halo(two, hlo.at[1, 0], [(p, COEFS[p + 1])])

        if p >= planes - REACH:
            @pl.when(has_up)
            def _():
                add_halo(two, hup.at[1, 0], [(p, COEFS[planes - p])])

        def step(s, carry, p=p):
            rows = rows_of(s, wide)
            start = src[p, rows, :]
            value = start - coef[0] * (two[p, rows, :] + squared * start)
            res[p, rows, :] = value
            return carry + value * value

        total_res = over(step, total_res)
        if p in order[:4]:
            send(2, p)
    post(1, total_res)
    for p in order[4:]:
        send(2, p)

    interior(res, fin)

    def direct(p, total):
        def step(s, carry):
            rows = rows_of(s, wide)
            value = res[p, rows, :] + coef[1] * src[p, rows, :]
            dirn[p, rows, :] = value
            return carry + value * value

        return over(step, total)

    def square_fin(p, total):
        def step(s, carry):
            rows = rows_of(s, wide)
            value = fin[p, rows, :] + coef[1] * img[p, rows, :]
            return carry + value * value

        return over(step, total)

    total_fin = zero
    done = list(range(REACH, planes - REACH))
    for p in done:
        share(1, fin, p)
    for k in range(REACH):
        if k == REACH - 2:
            await_sums(1)
            norm1 = collect(1, 0)
            ratio = norm1 / norm0
            keep(1, ratio)
            total_dir = lax.fori_loop(0, planes, direct, zero)
            for p in done:
                total_fin = square_fin(p, total_fin)
        arrive(2, k, fin)
        for p in (REACH - 1 - k, planes - REACH + k):
            done.append(p)
            share(1, fin, p)
            if k >= REACH - 2:
                total_fin = square_fin(p, total_fin)
    post(2, total_dir, total_fin)
    await_sums(2)
    step1 = norm1 / (collect(2, 1) + squared * collect(2, 0))
    keep(2, step1)

    mix[3, 0] = jnp.broadcast_to(-4.0 * (step0 + step1 * ratio), mix.shape[2:])
    mix[3, 1] = jnp.broadcast_to(-4.0 * step1, mix.shape[2:])

    def tell(slot):
        return pltpu.make_async_remote_copy(
            src_ref=mix.at[3], dst_ref=mix.at[slot],
            send_sem=mix_s.at[slot], recv_sem=mix_r.at[slot],
            device_id={"orb": quarters[slot]}, device_id_type=pl.DeviceIdType.MESH)

    for slot in range(3):
        tell(slot).start()

    def respond(slot, p):
        rows = rows_in(slot)
        return orb[p, rows, :] * (
            mix[3, 0, 0:1, :] * img[p, rows, :] + mix[3, 1, 0:1, :] * fin[p, rows, :])

    def hand(slot, c):
        return pltpu.make_async_remote_copy(
            src_ref=part.at[slot, c], dst_ref=got.at[slot, c],
            send_sem=part_s.at[slot, c], recv_sem=part_r.at[slot, c],
            device_id={"orb": first}, device_id_type=pl.DeviceIdType.MESH)

    def hand_last(c):
        return pltpu.make_async_remote_copy(
            src_ref=part.at[2, c], dst_ref=last.at[c],
            send_sem=last_s.at[c], recv_sem=last_r.at[c],
            device_id={"orb": second}, device_id_type=pl.DeviceIdType.MESH)

    for slot in (0, 1):
        for c, p in enumerate(outer):
            part[slot, c] = respond(slot, p)
            hand(slot, c).start()
    for c, p in enumerate(outer):
        part[2, c] = respond(2, p)
        dens[p] = respond(3, p)

    for k in range(REACH):
        @pl.when(has_low)
        def _():
            down(0, k).wait_send()

        @pl.when(has_up)
        def _():
            up(0, k).wait_send()

    def solve(p, carry):
        def step(s, inner):
            rows = rows_of(s, wide)
            src[p, rows, :] = coef[0] * src[p, rows, :] + coef[2] * dirn[p, rows, :]
            return inner

        return over(step, carry)

    lax.fori_loop(0, planes, solve, 0)

    for c in range(len(outer)):
        hand(0, c).wait_recv()
        part[2, c] = part[2, c] + got[0, c]
        hand_last(c).start()
    for slot in range(3):
        tell(slot).wait_recv()
    for p in middle:
        total = respond(3, p)
        for slot in range(3):
            for field in range(2):
                ship_copy(field, slot, p).wait_recv()
                total = total + mix[slot, field, 0:1, :] * land[field, slot, p - edge]
        dens[p] = total
    for c, p in enumerate(outer):
        hand(1, c).wait_recv()
        hand_last(c).wait_recv()
        dens[p] = dens[p] + (got[1, c] + last[c])

    for r in (1, 2):
        for k in range(REACH):
            @pl.when(has_low)
            def _():
                down(r, k).wait_send()

            @pl.when(has_up)
            def _():
                up(r, k).wait_send()
    for r in range(3):
        for j in range(1, n):
            exchange(r, j, g).wait_send()
    for slot in range(3):
        tell(slot).wait_send()
        for p in middle:
            ship_copy(0, slot, p).wait_send()
            ship_copy(1, slot, p).wait_send()
    for c in range(len(outer)):
        hand(0, c).wait_send()
        hand(1, c).wait_send()
        hand_last(c).wait_send()


def write_out(sol, den, sol_hbm, den_hbm, sem):
    copies = [
        pltpu.make_async_copy(sol, sol_hbm, sem.at[0]),
        pltpu.make_async_copy(den, den_hbm, sem.at[1]),
    ]
    for copy in copies:
        copy.start()
    for copy in copies:
        copy.wait()


def body(n, groups, orbitals, potential, trial_potential, eigenvalues, frequency):
    count, planes, ny, nz = orbitals.shape
    assert count == 1 and groups == 4 and planes >= 2 * REACH
    assert ny % 32 == 0 and nz % 128 == 0 and min(ny, nz) > 2 * REACH
    quarter = ny // groups
    wide = 32
    edge = planes // 6
    inner = planes - 2 * edge
    f32 = jnp.float32
    field = pltpu.VMEM((planes, ny, nz), f32)
    dma = pltpu.SemaphoreType.DMA
    anywhere = pl.BlockSpec(memory_space=pl.ANY)
    hbm = pl.BlockSpec(memory_space=pltpu.HBM)
    vmem = pl.BlockSpec(memory_space=pltpu.VMEM)
    sol, den = pl.pallas_call(
        functools.partial(kernel, n),
        out_shape=(
            pltpu.VMEM((planes, ny, nz), f32),
            pltpu.VMEM((planes, quarter, nz), f32),
        ),
        in_specs=[hbm] * 5,
        out_specs=(vmem, vmem),
        scratch_shapes=[field] * 8 + [
            pltpu.VMEM((2, nz, nz), jnp.bfloat16),
            pltpu.VMEM((2, ny, ny), jnp.bfloat16),
            pltpu.VMEM((3, REACH, ny, nz), f32),
            pltpu.VMEM((3, REACH, ny, nz), f32),
            pltpu.VMEM((3, n, 2, 8, 128), f32),
            pltpu.VMEM((3, wide, nz), f32),
            pltpu.VMEM((3, 2 * edge, quarter, nz), f32),
            pltpu.VMEM((2, 2 * edge, quarter, nz), f32),
            pltpu.VMEM((2 * edge, quarter, nz), f32),
            pltpu.VMEM((2, 3, inner, quarter, nz), f32),
            pltpu.VMEM((2, 3, inner, quarter, nz), f32),
            pltpu.VMEM((4, 2, 8, nz), f32),
            pltpu.SMEM((1,), f32), pltpu.SMEM((1,), f32),
            pltpu.SemaphoreType.REGULAR, pltpu.SemaphoreType.REGULAR,
            dma((2, planes)), dma((3,)),
            dma((3, REACH)), dma((3, REACH)), dma((3, REACH)), dma((3, REACH)),
            dma((3, n)), dma((3, n)),
            dma((2, 2 * edge)), dma((2, 2 * edge)), dma((2 * edge,)), dma((2 * edge,)),
            dma((2, 3, inner)), dma((2, 3, inner)), dma((3,)), dma((3,)),
        ],
        compiler_params=pltpu.CompilerParams(
            collective_id=0, has_side_effects=True, vmem_limit_bytes=50 * 2**20),
        name="sternheimer",
    )(
        orbitals.reshape(planes, ny, nz), potential, trial_potential,
        eigenvalues, frequency,
    )
    sol, den = pl.pallas_call(
        write_out,
        out_shape=(jax.ShapeDtypeStruct(sol.shape, f32), jax.ShapeDtypeStruct(den.shape, f32)),
        in_specs=[vmem] * 2,
        out_specs=(anywhere, anywhere),
        scratch_shapes=[dma((2,))],
        compiler_params=pltpu.CompilerParams(vmem_limit_bytes=2**20),
        name="write_out",
    )(sol, den)
    return sol.reshape(orbitals.shape), den


def solution(mesh):
    in_specs = (
        P("orb", "grid", None, None),
        P("grid", None, None),
        P("grid", None, None),
        P("orb"),
        P(),
    )
    out_specs = (P("orb", "grid", None, None), P("grid", "orb", None))
    call = functools.partial(body, mesh.shape["grid"], mesh.shape["orb"])
    return jax.shard_map(call, mesh=mesh, in_specs=in_specs, out_specs=out_specs, check_vma=False)
```

profile of v0, /device:TPU:9, one launch (start us, length us, event | category | flops | bytes accessed | tf_op | source)
XLA Modules:
  0.0 71.9 jit_solution(15981215351349502302)
XLA Ops:
  1.9 68.4 %sternheimer.1 = (f32[12,192,256]{2,1,0:T(8,128)S(1)}, f32[12,48,256]{2,1,0:T(8,128)S(1)}) custom-call(f32[12,192,256]{2,1,0:T(8,128)} %bitcast.2, f32[12,192,256]{2,1,0:T(8,128)} %pot_hbm.1, f32[12,192,256]{2,1,0:T(8,128)} %tri_hbm.1, f32[1]{0:T(128)S(6)} %copy.7.eig_hbm, f32[1]{0:T(128)S(6)} %copy.8.freq_hbm), custom_call_target="tpu_custom_call" | custom-call | tf_op jit(solution)/shard_map/sternheimer/pallas_call | solution.py:506
  70.3 1.6 %write_out.1 = (f32[12,192,256]{2,1,0:T(8,128)}, f32[12,48,256]{2,1,0:T(8,128)}) custom-call(f32[12,192,256]{2,1,0:T(8,128)S(1)} %get-tuple-element.6.sol, f32[12,48,256]{2,1,0:T(8,128)S(1)} %get-tuple-element.7.den), custom_call_target="tpu_custom_call" | custom-call | tf_op jit(solution)/shard_map/write_out/pallas_call | solution.py:542
where the time goes:
time: 72.1 us; the launch traced here: 71.9 us
  Pallas kernels  70 us (97%)
  between operations  1.93 us (3%)
    pallas_call x1, Pallas kernels, body(): pl.pallas_call(functools.partial(kernel, n), out_shape=(pltpu.VMEM((plane...  68.4 us
    pallas_call x1, Pallas kernels, body(): pl.pallas_call(write_out, out_shape=(jax.ShapeDtypeStruct(sol.shape, f32)...  1.61 us

commit v1 on v0

v1 whole, which is shorter than its diff:
```python
import functools

import jax
import jax.numpy as jnp
from jax import lax
from jax.experimental import pallas as pl
from jax.experimental.pallas import tpu as pltpu
from jax.sharding import PartitionSpec as P

STENCIL = (
    -5369.0 / 1800.0,
    12.0 / 7.0,
    -15.0 / 56.0,
    10.0 / 189.0,
    -1.0 / 112.0,
    2.0 / 1925.0,
    -1.0 / 16632.0,
)
SPACING = 0.75
REACH = len(STENCIL) - 1
COEFS = tuple(-0.5 / (SPACING * SPACING) * c for c in STENCIL)
STRIP = 8


def circulant(ref, count):
    size = ref.shape[1]

    def step(s, carry):
        rows = pl.ds(pl.multiple_of(s * count, count), count)
        row = s * count + lax.broadcasted_iota(jnp.int32, (count, size), 0)
        apart = jnp.abs(row - lax.broadcasted_iota(jnp.int32, (count, size), 1))
        apart = jnp.minimum(apart, size - apart)
        full = jnp.zeros((count, size), jnp.float32)
        for k in range(1, REACH + 1):
            full = jnp.where(apart == k, COEFS[k], full)
        high = full.astype(jnp.bfloat16)
        ref[0, rows, :] = high
        ref[1, rows, :] = (full - high.astype(jnp.float32)).astype(jnp.bfloat16)
        return carry

    lax.fori_loop(0, size // count, step, 0)


def kernel(
    n,
    orb_hbm, pot_hbm, tri_hbm, eig_hbm, freq_hbm,
    src, dens,
    orb, pot, tri, img, two, fin, cz, cy,
    hslow, hfast, sums, ship, land, ship_late, land_late, mix,
    eig, freq, ld_sem, mat_sem,
    slow_s, slow_r, fast_s, fast_r, sum_s, sum_r,
    ship_s, ship_r, late_s, late_r, mix_s, mix_r,
):
    planes, ny, nz = src.shape
    wide = 32
    late = ship_late.shape[1]
    quarter = ship.shape[3]
    g = lax.axis_index("grid")
    o = lax.axis_index("orb")
    odd = lax.rem(g, 2)
    slow_id = lax.rem(g + n - 1 + 2 * odd, n)
    fast_id = g + 1 - 2 * odd
    has_slow = jnp.logical_and(g + odd > 0, g + odd < n)
    flip1 = o + 1 - 2 * lax.rem(o, 2)
    flip2 = lax.rem(o + 2, 4)
    first = (1 - odd) * flip1 + odd * flip2
    second = odd * flip1 + (1 - odd) * flip2
    both = 3 - o
    quarters = (both, first, second, o)

    barrier = pltpu.get_barrier_semaphore()
    for j in range(1, n):
        pl.semaphore_signal(barrier, inc=1, device_id={"grid": lax.rem(g + j, n)})
    for slot in range(3):
        pl.semaphore_signal(barrier, inc=1, device_id={"orb": quarters[slot]})

    def at(d):
        return d + odd * (planes - 1 - 2 * d)

    def span(d, count):
        return pl.ds(d + odd * (planes - count - 2 * d), count)

    def load(which, d):
        hbm, ref = ((orb_hbm, orb), (tri_hbm, tri))[which]
        return pltpu.make_async_copy(hbm.at[at(d)], ref.at[at(d)], ld_sem.at[which, d])

    order = list(range(REACH)) + list(range(planes - 1, REACH - 1, -1))
    for d in order:
        load(0, d).start()
        load(1, d).start()
    mats = [
        pltpu.make_async_copy(pot_hbm, pot, mat_sem.at[0]),
        pltpu.make_async_copy(eig_hbm, eig, mat_sem.at[1]),
        pltpu.make_async_copy(freq_hbm, freq, mat_sem.at[2]),
    ]
    for copy in mats:
        copy.start()

    fields = (src, img, two)

    def slow(r, k):
        return pltpu.make_async_remote_copy(
            src_ref=fields[r].at[at(k)], dst_ref=hslow.at[r, k],
            send_sem=slow_s.at[r], recv_sem=slow_r.at[r, k],
            device_id={"grid": slow_id}, device_id_type=pl.DeviceIdType.MESH)

    def slow_sent(r):
        return pltpu.make_async_remote_copy(
            src_ref=fields[r].at[span(0, REACH)], dst_ref=hslow.at[r],
            send_sem=slow_s.at[r], recv_sem=slow_r.at[r, 0],
            device_id={"grid": slow_id}, device_id_type=pl.DeviceIdType.MESH)

    def fast(r):
        return pltpu.make_async_remote_copy(
            src_ref=fields[r].at[span(planes - REACH, REACH)], dst_ref=hfast.at[r],
            send_sem=fast_s.at[r], recv_sem=fast_r.at[r],
            device_id={"grid": fast_id}, device_id_type=pl.DeviceIdType.MESH)

    def send(r, *ks):
        @pl.when(has_slow)
        def _():
            for k in ks:
                slow(r, k).start()

    def rows_in(slot):
        return pl.ds(pl.multiple_of(quarters[slot] * quarter, 8), quarter)

    def rows_of(s, count):
        return pl.ds(pl.multiple_of(s * count, count), count)

    def over(step, init, count=wide):
        return lax.fori_loop(0, ny // count, step, init)

    def ship_copy(field, slot, d, count, sem):
        piece = pl.ds(d - late, count)
        return pltpu.make_async_remote_copy(
            src_ref=ship.at[field, slot, piece], dst_ref=land.at[field, slot, piece],
            send_sem=ship_s, recv_sem=ship_r.at[field, slot, sem],
            device_id={"orb": quarters[slot]}, device_id_type=pl.DeviceIdType.MESH)

    batches = (
        ((REACH, planes - REACH), (late, REACH - late)),
        ((REACH, planes - REACH),) + tuple((d, 1) for d in range(REACH - 1, late - 1, -1)),
    )

    def share(field, value, batch):
        d, count = batches[field][batch]
        for slot in range(3):
            rows = rows_in(slot)
            for e in range(d, d + count):
                ship[field, slot, e - late] = orb[at(e), rows, :] * value[at(e), rows, :]
            ship_copy(field, slot, d, count, batch).start()

    zero = jnp.zeros((wide, nz), jnp.float32)

    def arrive(r, ks, acc):
        @pl.when(has_slow)
        def _():
            for k in ks:
                slow(r, k).wait_recv()

            def step(s, carry):
                rows = rows_of(s, wide)
                values = [hslow[r, k, rows, :] for k in ks]
                for d in range(REACH):
                    terms = [COEFS[d + 1 + k] * v for k, v in zip(ks, values) if d + k < REACH]
                    if terms:
                        acc[at(d), rows, :] = acc[at(d), rows, :] + functools.reduce(jnp.add, terms)
                return carry

            over(step, 0)

    def square_of(ref, d, total):
        def step(s, carry):
            value = ref[at(d), rows_of(s, wide), :]
            return carry + value * value

        return over(step, total)

    def across(value, out, low, high):
        def plane(d, carry):
            p = at(d)
            whole = value[p]
            high_part = whole.astype(jnp.bfloat16)
            low_part = (whole - high_part.astype(jnp.float32)).astype(jnp.bfloat16)
            product = functools.partial(jnp.dot, preferred_element_type=jnp.float32)
            along_z = product(high_part, cz[0]) + product(low_part, cz[0]) + product(high_part, cz[1])
            along_y = product(cy[0], high_part) + product(cy[0], low_part) + product(cy[1], high_part)
            out[p] = along_z + along_y
            return carry

        lax.fori_loop(low, high, plane, 0)

    def along(r, value, out):
        fast(r).wait_recv()

        def strip(s, carry):
            rows = rows_of(s, STRIP)
            parts = [value[at(d), rows, :] for d in range(planes)]
            parts += [hfast[r, k + odd * (REACH - 1 - 2 * k), rows, :] for k in range(REACH)]
            for d in range(planes):
                total = out[at(d), rows, :] + (pot[at(d), rows, :] + (3.0 * COEFS[0] - energy)) * parts[d]
                for k in range(1, REACH + 1):
                    near = [parts[e] for e in (d - k, d + k) if 0 <= e < planes + REACH]
                    total = total + COEFS[k] * (near[0] + near[1] if len(near) == 2 else near[0])
                out[at(d), rows, :] = total
            return carry

        over(strip, 0, STRIP)

    def fold(total):
        total = functools.reduce(
            lambda a, b: a + b, [total[i:i + 8] for i in range(0, wide, 8)])
        total = functools.reduce(
            lambda a, b: a + b, [total[:, i:i + 128] for i in range(0, nz, 128)])
        return jnp.sum(total, axis=0, keepdims=True)

    def exchange(r, j, slot):
        return pltpu.make_async_remote_copy(
            src_ref=sums.at[r, slot], dst_ref=sums.at[r, slot],
            send_sem=sum_s.at[r], recv_sem=sum_r.at[r],
            device_id={"grid": lax.rem(g + j, n)}, device_id_type=pl.DeviceIdType.MESH)

    def exchanged(r):
        return pltpu.make_async_remote_copy(
            src_ref=sums.at[r, pl.ds(0, n - 1)], dst_ref=sums.at[r, pl.ds(0, n - 1)],
            send_sem=sum_s.at[r], recv_sem=sum_r.at[r],
            device_id={"grid": fast_id}, device_id_type=pl.DeviceIdType.MESH)

    def post(r, *totals):
        for i in range(2):
            row = fold(totals[i]) if i < len(totals) else jnp.zeros((1, 128), jnp.float32)
            sums[r, g, i:i + 1, :] = row
        for j in range(1, n):
            exchange(r, j, g).start()

    def collect(r):
        exchanged(r).wait_recv()
        total = sums[r, 0]
        for m in range(1, n):
            total = total + sums[r, m]
        return tuple(jnp.sum(total[i:i + 1], keepdims=True) for i in range(2))

    def spread(value):
        return jnp.broadcast_to(value, (1, nz))

    circulant(cz, 32)
    circulant(cy, 32)

    total_src = zero
    for d in order:
        load(0, d).wait()
        load(1, d).wait()

        def step(s, carry, d=d):
            rows = rows_of(s, wide)
            value = orb[at(d), rows, :] * tri[at(d), rows, :]
            src[at(d), rows, :] = value
            return carry + value * value

        total_src = over(step, total_src)
        if d == order[0]:
            pl.semaphore_wait(barrier, n + 2)
        if d < REACH:
            send(0, d)
    fast(0).start()
    for copy in mats:
        copy.wait()
    energy = eig[0]
    squared = freq[0] * freq[0]

    across(src, img, 0, planes)
    along(0, src, img)
    fast(1).start()
    share(0, img, 0)
    total_img = zero
    for d in range(REACH, planes):
        total_img = square_of(img, d, total_img)
    early = list(range(REACH - late))
    arrive(0, early, img)
    send(1, REACH - 1)
    share(0, img, 1)
    for k in early:
        total_img = square_of(img, REACH - 1 - k, total_img)
    across(img, two, late, planes)
    for k in range(REACH - late, REACH):
        arrive(0, [k], img)
        total_img = square_of(img, REACH - 1 - k, total_img)
        if k < REACH - 1:
            across(img, two, REACH - 1 - k, REACH - k)
    post(0, total_src, total_img)
    send(1, *range(REACH - 1))
    across(img, two, 0, 1)
    along(1, img, two)
    fast(2).start()

    across(two, fin, REACH, planes)
    arrive(1, [REACH - 1, 0], two)
    send(2, REACH - 1)
    across(two, fin, REACH - 1, REACH)
    norm0, form0 = collect(0)
    step0 = norm0 / (form0 + squared * norm0)
    back = spread(1.0 - step0 * squared)
    step0_row = spread(step0)

    def square_res(d, total):
        def step(s, carry):
            rows = rows_of(s, wide)
            value = back * src[at(d), rows, :] - step0_row * two[at(d), rows, :]
            return carry + value * value

        return over(step, total)

    total_res = zero
    for d in range(REACH - 1, planes):
        total_res = square_res(d, total_res)
    for k in range(1, REACH - 1):
        arrive(1, [k], two)
        total_res = square_res(REACH - 1 - k, total_res)
        if k < REACH - 2:
            across(two, fin, REACH - 1 - k, REACH - k)
    total_res = square_res(0, total_res)
    post(1, total_res)
    send(2, *range(REACH - 1))
    across(two, fin, 0, 2)
    along(2, two, fin)
    share(1, fin, 0)
    arrive(2, [REACH - 1, 0], fin)
    share(1, fin, 1)

    norm1, _ = collect(1)
    ratio = norm1 / norm0
    keep = 1.0 - step0 * squared + ratio
    keep_row = spread(keep)

    def square_dir(d, total):
        def step(s, carry):
            rows = rows_of(s, wide)
            value = keep_row * src[at(d), rows, :] - step0_row * two[at(d), rows, :]
            return carry + value * value

        return over(step, total)

    def square_fin(d, total):
        def step(s, carry):
            rows = rows_of(s, wide)
            value = keep_row * img[at(d), rows, :] - step0_row * fin[at(d), rows, :]
            return carry + value * value

        return over(step, total)

    def loop_over(low, high, body, total):
        return lax.fori_loop(low, high, body, total)

    total_dir = loop_over(0, planes, square_dir, zero)
    total_fin = loop_over(REACH - 1, planes, square_fin, zero)
    for k in range(1, REACH - 1):
        arrive(2, [k], fin)
        if REACH - 1 - k >= late:
            share(1, fin, k + 1)
        total_fin = square_fin(REACH - 1 - k, total_fin)
    total_fin = square_fin(0, total_fin)
    post(2, total_dir, total_fin)
    form_dir, form_fin = collect(2)
    step1 = norm1 / (form_fin + squared * form_dir)

    near_img = -4.0 * (step0 + step1 * keep)
    near_fin = 4.0 * (step1 * step0)
    mix[3, 0] = jnp.broadcast_to(near_img, mix.shape[2:])
    mix[3, 1] = jnp.broadcast_to(near_fin, mix.shape[2:])

    def tell(slot):
        return pltpu.make_async_remote_copy(
            src_ref=mix.at[3], dst_ref=mix.at[slot],
            send_sem=mix_s.at[slot], recv_sem=mix_r.at[slot],
            device_id={"orb": quarters[slot]}, device_id_type=pl.DeviceIdType.MESH)

    near_img_row = spread(near_img)
    near_fin_row = spread(near_fin)

    def respond(slot, d):
        rows = rows_in(slot)
        return orb[at(d), rows, :] * (
            near_img_row * img[at(d), rows, :] + near_fin_row * fin[at(d), rows, :])

    def late_copy(slot):
        return pltpu.make_async_remote_copy(
            src_ref=ship_late.at[slot], dst_ref=land_late.at[slot],
            send_sem=late_s.at[slot], recv_sem=late_r.at[slot],
            device_id={"orb": quarters[slot]}, device_id_type=pl.DeviceIdType.MESH)

    for slot in range(3):
        for d in range(late):
            ship_late[slot, d] = respond(slot, d)
        tell(slot).start()
        late_copy(slot).start()

    @pl.when(has_slow)
    def _():
        slow_sent(0).wait_send()

    fast(0).wait_send()
    sol_src = spread(step0 + step1 * keep)
    sol_two = spread(step1 * step0)

    def solve(p, carry):
        def step(s, inner):
            rows = rows_of(s, wide)
            src[p, rows, :] = sol_src * src[p, rows, :] - sol_two * two[p, rows, :]
            return inner

        return over(step, carry)

    lax.fori_loop(0, planes, solve, 0)
    for d in range(planes):
        dens[at(d)] = respond(3, d)
    for slot in range(3):
        tell(slot).wait_recv()
    for batch, (d, count) in enumerate(batches[0]):
        for slot in range(3):
            ship_copy(0, slot, d, count, batch).wait_recv()
    for batch, (d, count) in enumerate(batches[1]):
        for slot in range(3):
            ship_copy(1, slot, d, count, batch).wait_recv()
        for e in range(d, d + count):
            total = dens[at(e)]
            for slot in range(3):
                for field in range(2):
                    total = total + mix[slot, field, 0:1, :] * land[field, slot, e - late]
            dens[at(e)] = total
    for slot in range(3):
        late_copy(slot).wait_recv()
    for d in range(late):
        dens[at(d)] = dens[at(d)] + (land_late[0, d] + land_late[1, d] + land_late[2, d])

    @pl.when(has_slow)
    def _():
        slow_sent(1).wait_send()
        slow_sent(2).wait_send()

    fast(1).wait_send()
    fast(2).wait_send()
    for r in range(3):
        exchanged(r).wait_send()
    pltpu.make_async_remote_copy(
        src_ref=ship, dst_ref=land, send_sem=ship_s, recv_sem=ship_r.at[0, 0, 0],
        device_id={"orb": both}, device_id_type=pl.DeviceIdType.MESH).wait_send()
    for slot in range(3):
        tell(slot).wait_send()
        late_copy(slot).wait_send()


def write_out(sol, den, sol_hbm, den_hbm, sem):
    copies = [
        pltpu.make_async_copy(sol, sol_hbm, sem.at[0]),
        pltpu.make_async_copy(den, den_hbm, sem.at[1]),
    ]
    for copy in copies:
        copy.start()
    for copy in copies:
        copy.wait()


def body(n, groups, orbitals, potential, trial_potential, eigenvalues, frequency):
    count, planes, ny, nz = orbitals.shape
    assert count == 1 and groups == 4 and n % 2 == 0
    assert planes >= 2 * REACH and planes // 4 < REACH
    assert ny % 32 == 0 and nz % 128 == 0 and min(ny, nz) > 2 * REACH
    quarter = ny // groups
    late = planes // 4
    early = planes - late
    f32 = jnp.float32
    field = pltpu.VMEM((planes, ny, nz), f32)
    dma = pltpu.SemaphoreType.DMA
    anywhere = pl.BlockSpec(memory_space=pl.ANY)
    hbm = pl.BlockSpec(memory_space=pltpu.HBM)
    vmem = pl.BlockSpec(memory_space=pltpu.VMEM)
    sol, den = pl.pallas_call(
        functools.partial(kernel, n),
        out_shape=(
            pltpu.VMEM((planes, ny, nz), f32),
            pltpu.VMEM((planes, quarter, nz), f32),
        ),
        in_specs=[hbm] * 5,
        out_specs=(vmem, vmem),
        scratch_shapes=[field] * 6 + [
            pltpu.VMEM((2, nz, nz), jnp.bfloat16),
            pltpu.VMEM((2, ny, ny), jnp.bfloat16),
            pltpu.VMEM((3, REACH, ny, nz), f32),
            pltpu.VMEM((3, REACH, ny, nz), f32),
            pltpu.VMEM((3, n, 2, 128), f32),
            pltpu.VMEM((2, 3, early, quarter, nz), f32),
            pltpu.VMEM((2, 3, early, quarter, nz), f32),
            pltpu.VMEM((3, late, quarter, nz), f32),
            pltpu.VMEM((3, late, quarter, nz), f32),
            pltpu.VMEM((4, 2, 8, nz), f32),
            pltpu.SMEM((1,), f32), pltpu.SMEM((1,), f32),
            dma((2, planes)), dma((3,)),
            dma((3,)), dma((3, REACH)), dma((3,)), dma((3,)), dma((3,)), dma((3,)),
            dma(()), dma((2, 3, 1 + REACH)), dma((3,)), dma((3,)), dma((3,)), dma((3,)),
        ],
        compiler_params=pltpu.CompilerParams(
            collective_id=0, has_side_effects=True, vmem_limit_bytes=50 * 2**20),
        name="sternheimer",
    )(
        orbitals.reshape(planes, ny, nz), potential, trial_potential,
        eigenvalues, frequency,
    )
    sol, den = pl.pallas_call(
        write_out,
        out_shape=(jax.ShapeDtypeStruct(sol.shape, f32), jax.ShapeDtypeStruct(den.shape, f32)),
        in_specs=[vmem] * 2,
        out_specs=(anywhere, anywhere),
        scratch_shapes=[dma((2,))],
        compiler_params=pltpu.CompilerParams(vmem_limit_bytes=2**20),
        name="write_out",
    )(sol, den)
    return sol.reshape(orbitals.shape), den


def solution(mesh):
    in_specs = (
        P("orb", "grid", None, None),
        P("grid", None, None),
        P("grid", None, None),
        P("orb"),
        P(),
    )
    out_specs = (P("orb", "grid", None, None), P("grid", "orb", None))
    call = functools.partial(body, mesh.shape["grid"], mesh.shape["orb"])
    return jax.shard_map(call, mesh=mesh, in_specs=in_specs, out_specs=out_specs, check_vma=False)
```

time: 72.1 us -> 67.7 us (0.939)
  the two profiles are of different devices: /device:TPU:9 before, /device:TPU:11 now
where the time goes in v1:
time: 67.7 us; the launch traced here: 67.6 us
  Pallas kernels  65.6 us (97%)
  between operations  1.93 us (3%)
    pallas_call x1, Pallas kernels, body(): pl.pallas_call(functools.partial(kernel, n), out_shape=(pltpu.VMEM((plane...  64 us
    pallas_call x1, Pallas kernels, body(): pl.pallas_call(write_out, out_shape=(jax.ShapeDtypeStruct(sol.shape, f32)...  1.61 us

profile of v1, /device:TPU:11, one launch (start us, length us, event | category | flops | bytes accessed | tf_op | source)
XLA Modules:
  0.0 67.6 jit_solution(11503344312869884575)
XLA Ops:
  1.9 64.0 %sternheimer.1 = (f32[12,192,256]{2,1,0:T(8,128)S(1)}, f32[12,48,256]{2,1,0:T(8,128)S(1)}) custom-call(f32[12,192,256]{2,1,0:T(8,128)} %bitcast.2, f32[12,192,256]{2,1,0:T(8,128)} %pot_hbm.1, f32[12,192,256]{2,1,0:T(8,128)} %tri_hbm.1, f32[1]{0:T(128)S(6)} %copy.7.eig_hbm, f32[1]{0:T(128)S(6)} %copy.8.freq_hbm), custom_call_target="tpu_custom_call" | custom-call | tf_op jit(solution)/shard_map/sternheimer/pallas_call | solution.py:478
  66.0 1.6 %write_out.1 = (f32[12,192,256]{2,1,0:T(8,128)}, f32[12,48,256]{2,1,0:T(8,128)}) custom-call(f32[12,192,256]{2,1,0:T(8,128)S(1)} %get-tuple-element.6.sol, f32[12,48,256]{2,1,0:T(8,128)S(1)} %get-tuple-element.7.den), custom_call_target="tpu_custom_call" | custom-call | tf_op jit(solution)/shard_map/write_out/pallas_call | solution.py:509

commit v2 on v1

--- a/solution.py
+++ b/solution.py
@@ -47,7 +47,7 @@
     src, dens,
     orb, pot, tri, img, two, fin, cz, cy,
     hslow, hfast, sums, ship, land, ship_late, land_late, mix,
-    eig, freq, ld_sem, mat_sem,
+    eig, freq, met, ld_sem, mat_sem,
     slow_s, slow_r, fast_s, fast_r, sum_s, sum_r,
     ship_s, ship_r, late_s, late_r, mix_s, mix_r,
 ):
@@ -69,8 +69,11 @@
     quarters = (both, first, second, o)
 
     barrier = pltpu.get_barrier_semaphore()
-    for j in range(1, n):
-        pl.semaphore_signal(barrier, inc=1, device_id={"grid": lax.rem(g + j, n)})
+    @pl.when(has_slow)
+    def _():
+        pl.semaphore_signal(barrier, inc=1, device_id={"grid": slow_id})
+
+    pl.semaphore_signal(barrier, inc=1, device_id={"grid": fast_id})
     for slot in range(3):
         pl.semaphore_signal(barrier, inc=1, device_id={"orb": quarters[slot]})
 
@@ -79,6 +82,20 @@
 
     def span(d, count):
         return pl.ds(d + odd * (planes - count - 2 * d), count)
+
+    def meet(i):
+        reach = 2 ** i
+        for peer in (g - reach, g + reach):
+            @pl.when(jnp.logical_and(peer >= 0, peer < n))
+            def _():
+                pl.semaphore_signal(met.at[i], inc=1, device_id={"grid": peer})
+
+    def met_by(i):
+        reach = 2 ** i
+        pl.semaphore_wait(
+            met.at[i], jnp.where(g >= reach, 1, 0) + jnp.where(g + reach < n, 1, 0))
+
+    rounds = met.shape[0]
 
     def load(which, d):
         hbm, ref = ((orb_hbm, orb), (tri_hbm, tri))[which]
@@ -138,9 +155,12 @@
             send_sem=ship_s, recv_sem=ship_r.at[field, slot, sem],
             device_id={"orb": quarters[slot]}, device_id_type=pl.DeviceIdType.MESH)
 
+    cut = REACH + late
+    lead = [REACH - 1, REACH - 2]
+    rest = list(range(REACH - 2))
     batches = (
         ((REACH, planes - REACH), (late, REACH - late)),
-        ((REACH, planes - REACH),) + tuple((d, 1) for d in range(REACH - 1, late - 1, -1)),
+        ((cut, planes - cut), (REACH, cut - REACH)) + tuple((d, 1) for d in range(REACH - 1, late - 1, -1)),
     )
 
     def share(field, value, batch):
@@ -178,7 +198,7 @@
         return over(step, total)
 
     def across(value, out, low, high):
-        def plane(d, carry):
+        def plane(d):
             p = at(d)
             whole = value[p]
             high_part = whole.astype(jnp.bfloat16)
@@ -187,26 +207,47 @@
             along_z = product(high_part, cz[0]) + product(low_part, cz[0]) + product(high_part, cz[1])
             along_y = product(cy[0], high_part) + product(cy[0], low_part) + product(cy[1], high_part)
             out[p] = along_z + along_y
+
+        count = high - low
+        size = max(k for k in range(1, REACH + 1) if count % k == 0)
+
+        def group(i, carry):
+            for j in range(size):
+                plane(low + i * size + j)
             return carry
 
-        lax.fori_loop(low, high, plane, 0)
-
-    def along(r, value, out):
-        fast(r).wait_recv()
-
-        def strip(s, carry):
-            rows = rows_of(s, STRIP)
-            parts = [value[at(d), rows, :] for d in range(planes)]
-            parts += [hfast[r, k + odd * (REACH - 1 - 2 * k), rows, :] for k in range(REACH)]
-            for d in range(planes):
-                total = out[at(d), rows, :] + (pot[at(d), rows, :] + (3.0 * COEFS[0] - energy)) * parts[d]
-                for k in range(1, REACH + 1):
-                    near = [parts[e] for e in (d - k, d + k) if 0 <= e < planes + REACH]
-                    total = total + COEFS[k] * (near[0] + near[1] if len(near) == 2 else near[0])
-                out[at(d), rows, :] = total
-            return carry
-
-        over(strip, 0, STRIP)
+        lax.fori_loop(0, count // size, group, 0)
+
+    def along(r, value, out, low, high):
+        for side in (0, 1):
+            @pl.when(odd == side)
+            def _(side=side):
+                def place(d):
+                    return planes - 1 - d if side else d
+
+                def part(d, rows):
+                    if d < planes:
+                        return value[place(d), rows, :]
+                    k = d - planes
+                    return hfast[r, REACH - 1 - k if side else k, rows, :]
+
+                def strip(s, carry):
+                    rows = rows_of(s, STRIP)
+                    parts = {
+                        d: part(d, rows)
+                        for d in range(max(0, low - REACH), min(planes, high) + REACH)
+                        if d < high + REACH
+                    }
+                    for d in range(low, high):
+                        here = out.at[place(d), rows, :]
+                        total = here[...] + (pot[place(d), rows, :] + (3.0 * COEFS[0] - energy)) * parts[d]
+                        for k in range(1, REACH + 1):
+                            near = [parts[e] for e in (d - k, d + k) if e in parts]
+                            total = total + COEFS[k] * (near[0] + near[1] if len(near) == 2 else near[0])
+                        here[...] = total
+                    return carry
+
+                over(strip, 0, STRIP)
 
     def fold(total):
         total = functools.reduce(
@@ -260,7 +301,8 @@
 
         total_src = over(step, total_src)
         if d == order[0]:
-            pl.semaphore_wait(barrier, n + 2)
+            pl.semaphore_wait(barrier, 4 + has_slow.astype(jnp.int32))
+            meet(0)
         if d < REACH:
             send(0, d)
     fast(0).start()
@@ -269,16 +311,25 @@
     energy = eig[0]
     squared = freq[0] * freq[0]
 
-    across(src, img, 0, planes)
-    along(0, src, img)
+    across(src, img, REACH, planes)
+    if rounds > 1:
+        met_by(0)
+        meet(1)
+    fast(0).wait_recv()
+    along(0, src, img, REACH, planes)
     fast(1).start()
     share(0, img, 0)
+    across(src, img, 0, REACH)
+    along(0, src, img, 0, REACH)
+    for i in range(1, rounds - 1):
+        met_by(i)
+        meet(i + 1)
     total_img = zero
     for d in range(REACH, planes):
         total_img = square_of(img, d, total_img)
     early = list(range(REACH - late))
     arrive(0, early, img)
-    send(1, REACH - 1)
+    send(1, *lead)
     share(0, img, 1)
     for k in early:
         total_img = square_of(img, REACH - 1 - k, total_img)
@@ -288,14 +339,16 @@
         total_img = square_of(img, REACH - 1 - k, total_img)
         if k < REACH - 1:
             across(img, two, REACH - 1 - k, REACH - k)
+    met_by(rounds - 1)
     post(0, total_src, total_img)
-    send(1, *range(REACH - 1))
+    send(1, *rest)
     across(img, two, 0, 1)
-    along(1, img, two)
+    fast(1).wait_recv()
+    along(1, img, two, 0, planes)
     fast(2).start()
 
     across(two, fin, REACH, planes)
-    arrive(1, [REACH - 1, 0], two)
+    arrive(1, [*lead, 0], two)
     send(2, REACH - 1)
     across(two, fin, REACH - 1, REACH)
     norm0, form0 = collect(0)
@@ -314,19 +367,27 @@
     total_res = zero
     for d in range(REACH - 1, planes):
         total_res = square_res(d, total_res)
-    for k in range(1, REACH - 1):
+    for k in range(1, REACH - late):
         arrive(1, [k], two)
-        total_res = square_res(REACH - 1 - k, total_res)
-        if k < REACH - 2:
-            across(two, fin, REACH - 1 - k, REACH - k)
-    total_res = square_res(0, total_res)
+        d = REACH - 1 - k
+        if d in lead:
+            send(2, d)
+        total_res = square_res(d, total_res)
+        across(two, fin, d, d + 1)
+    fast(2).wait_recv()
+    along(2, two, fin, cut, planes)
+    share(1, fin, 0)
+    for k in range(REACH - late, rest[-1] + 1):
+        arrive(1, [k], two)
+    for d in range(late):
+        total_res = square_res(d, total_res)
     post(1, total_res)
-    send(2, *range(REACH - 1))
-    across(two, fin, 0, 2)
-    along(2, two, fin)
-    share(1, fin, 0)
-    arrive(2, [REACH - 1, 0], fin)
+    send(2, *rest)
+    across(two, fin, 0, late)
+    along(2, two, fin, 0, cut)
     share(1, fin, 1)
+    arrive(2, [*lead, 0], fin)
+    share(1, fin, 2)
 
     norm1, _ = collect(1)
     ratio = norm1 / norm0
@@ -354,12 +415,13 @@
 
     total_dir = loop_over(0, planes, square_dir, zero)
     total_fin = loop_over(REACH - 1, planes, square_fin, zero)
-    for k in range(1, REACH - 1):
+    for k in rest[1:]:
         arrive(2, [k], fin)
         if REACH - 1 - k >= late:
-            share(1, fin, k + 1)
-        total_fin = square_fin(REACH - 1 - k, total_fin)
-    total_fin = square_fin(0, total_fin)
+            share(1, fin, k + 2)
+            total_fin = square_fin(REACH - 1 - k, total_fin)
+    for d in range(late):
+        total_fin = square_fin(d, total_fin)
     post(2, total_dir, total_fin)
     form_dir, form_fin = collect(2)
     step1 = norm1 / (form_fin + squared * form_dir)
@@ -464,10 +526,10 @@
 def body(n, groups, orbitals, potential, trial_potential, eigenvalues, frequency):
     count, planes, ny, nz = orbitals.shape
     assert count == 1 and groups == 4 and n % 2 == 0
-    assert planes >= 2 * REACH and planes // 4 < REACH
+    assert planes >= 2 * REACH
     assert ny % 32 == 0 and nz % 128 == 0 and min(ny, nz) > 2 * REACH
     quarter = ny // groups
-    late = planes // 4
+    late = REACH // 2
     early = planes - late
     f32 = jnp.float32
     field = pltpu.VMEM((planes, ny, nz), f32)
@@ -495,9 +557,10 @@
             pltpu.VMEM((3, late, quarter, nz), f32),
             pltpu.VMEM((4, 2, 8, nz), f32),
             pltpu.SMEM((1,), f32), pltpu.SMEM((1,), f32),
+            pltpu.SemaphoreType.REGULAR(((n - 1).bit_length(),)),
             dma((2, planes)), dma((3,)),
             dma((3,)), dma((3, REACH)), dma((3,)), dma((3,)), dma((3,)), dma((3,)),
-            dma(()), dma((2, 3, 1 + REACH)), dma((3,)), dma((3,)), dma((3,)), dma((3,)),
+            dma(()), dma((2, 3, 2 + REACH)), dma((3,)), dma((3,)), dma((3,)), dma((3,)),
         ],
         compiler_params=pltpu.CompilerParams(
             collective_id=0, has_side_effects=True, vmem_limit_bytes=50 * 2**20),

time: 67.7 us -> 62.9 us (0.929)
  the two profiles are of different devices: /device:TPU:11 before, /device:TPU:0 now
where the time goes in v2:
time: 62.9 us; the launch traced here: 62.7 us
  Pallas kernels  60.8 us (97%)
  between operations  1.93 us (3%)
    pallas_call x1, Pallas kernels, body(): pl.pallas_call(functools.partial(kernel, n), out_shape=(pltpu.VMEM((plane...  59.2 us
    pallas_call x1, Pallas kernels, body(): pl.pallas_call(write_out, out_shape=(jax.ShapeDtypeStruct(sol.shape, f32)...  1.61 us

profile of v2, /device:TPU:0, one launch (start us, length us, event | category | flops | bytes accessed | tf_op | source)
XLA Modules:
  0.0 62.7 jit_solution(17961129019278298270)
XLA Ops:
  1.9 59.2 %sternheimer.1 = (f32[12,192,256]{2,1,0:T(8,128)S(1)}, f32[12,48,256]{2,1,0:T(8,128)S(1)}) custom-call(f32[12,192,256]{2,1,0:T(8,128)} %bitcast.2, f32[12,192,256]{2,1,0:T(8,128)} %pot_hbm.1, f32[12,192,256]{2,1,0:T(8,128)} %tri_hbm.1, f32[1]{0:T(128)S(6)} %copy.7.eig_hbm, f32[1]{0:T(128)S(6)} %copy.8.freq_hbm), custom_call_target="tpu_custom_call" | custom-call | tf_op jit(solution)/shard_map/sternheimer/pallas_call | solution.py:540
  61.1 1.6 %write_out.1 = (f32[12,192,256]{2,1,0:T(8,128)}, f32[12,48,256]{2,1,0:T(8,128)}) custom-call(f32[12,192,256]{2,1,0:T(8,128)S(1)} %get-tuple-element.6.sol, f32[12,48,256]{2,1,0:T(8,128)S(1)} %get-tuple-element.7.den), custom_call_target="tpu_custom_call" | custom-call | tf_op jit(solution)/shard_map/write_out/pallas_call | solution.py:572

commit v3 on v2

--- a/solution.py
+++ b/solution.py
@@ -127,11 +127,28 @@
             send_sem=slow_s.at[r], recv_sem=slow_r.at[r, 0],
             device_id={"grid": slow_id}, device_id_type=pl.DeviceIdType.MESH)
 
-    def fast(r):
-        return pltpu.make_async_remote_copy(
+    half = REACH // 2
+
+    def fast(r, i):
+        return pltpu.make_async_remote_copy(
+            src_ref=fields[r].at[span(planes - half * (i + 1), half)],
+            dst_ref=hfast.at[r, pl.ds(half * (1 - i) + odd * half * (2 * i - 1), half)],
+            send_sem=fast_s.at[r], recv_sem=fast_r.at[r, i],
+            device_id={"grid": fast_id}, device_id_type=pl.DeviceIdType.MESH)
+
+    def fast_send(r):
+        fast(r, 0).start()
+        fast(r, 1).start()
+
+    def fast_wait(r):
+        fast(r, 0).wait_recv()
+        fast(r, 1).wait_recv()
+
+    def fast_sent(r):
+        pltpu.make_async_remote_copy(
             src_ref=fields[r].at[span(planes - REACH, REACH)], dst_ref=hfast.at[r],
-            send_sem=fast_s.at[r], recv_sem=fast_r.at[r],
-            device_id={"grid": fast_id}, device_id_type=pl.DeviceIdType.MESH)
+            send_sem=fast_s.at[r], recv_sem=fast_r.at[r, 0],
+            device_id={"grid": fast_id}, device_id_type=pl.DeviceIdType.MESH).wait_send()
 
     def send(r, *ks):
         @pl.when(has_slow)
@@ -155,12 +172,15 @@
             send_sem=ship_s, recv_sem=ship_r.at[field, slot, sem],
             device_id={"orb": quarters[slot]}, device_id_type=pl.DeviceIdType.MESH)
 
-    cut = REACH + late
+    cut = 2 * REACH - half
     lead = [REACH - 1, REACH - 2]
     rest = list(range(REACH - 2))
     batches = (
         ((REACH, planes - REACH), (late, REACH - late)),
-        ((cut, planes - cut), (REACH, cut - REACH)) + tuple((d, 1) for d in range(REACH - 1, late - 1, -1)),
+        ((2 * REACH - 1, planes - 2 * REACH + 1),)
+        + tuple((d, 1) for d in range(2 * REACH - 2, cut - 1, -1))
+        + ((REACH, cut - REACH),)
+        + tuple((d, 1) for d in range(REACH - 1, late - 1, -1)),
     )
 
     def share(field, value, batch):
@@ -305,7 +325,10 @@
             meet(0)
         if d < REACH:
             send(0, d)
-    fast(0).start()
+        if d == planes - half:
+            fast(0, 0).start()
+        if d == planes - REACH:
+            fast(0, 1).start()
     for copy in mats:
         copy.wait()
     energy = eig[0]
@@ -315,9 +338,9 @@
     if rounds > 1:
         met_by(0)
         meet(1)
-    fast(0).wait_recv()
+    fast_wait(0)
     along(0, src, img, REACH, planes)
-    fast(1).start()
+    fast_send(1)
     share(0, img, 0)
     across(src, img, 0, REACH)
     along(0, src, img, 0, REACH)
@@ -343,14 +366,17 @@
     post(0, total_src, total_img)
     send(1, *rest)
     across(img, two, 0, 1)
-    fast(1).wait_recv()
+    fast_wait(1)
     along(1, img, two, 0, planes)
-    fast(2).start()
+    fast_send(2)
 
     across(two, fin, REACH, planes)
+    fast_wait(2)
     arrive(1, [*lead, 0], two)
     send(2, REACH - 1)
     across(two, fin, REACH - 1, REACH)
+    along(2, two, fin, 2 * REACH - 1, planes)
+    share(1, fin, 0)
     norm0, form0 = collect(0)
     step0 = norm0 / (form0 + squared * norm0)
     back = spread(1.0 - step0 * squared)
@@ -367,27 +393,26 @@
     total_res = zero
     for d in range(REACH - 1, planes):
         total_res = square_res(d, total_res)
-    for k in range(1, REACH - late):
+    for k in range(1, half):
         arrive(1, [k], two)
         d = REACH - 1 - k
         if d in lead:
             send(2, d)
+        across(two, fin, d, d + 1)
+        along(2, two, fin, REACH + d, REACH + d + 1)
+        share(1, fin, k)
         total_res = square_res(d, total_res)
-        across(two, fin, d, d + 1)
-    fast(2).wait_recv()
-    along(2, two, fin, cut, planes)
-    share(1, fin, 0)
-    for k in range(REACH - late, rest[-1] + 1):
+    for k in range(half, rest[-1] + 1):
         arrive(1, [k], two)
-    for d in range(late):
+    for d in range(half):
         total_res = square_res(d, total_res)
     post(1, total_res)
     send(2, *rest)
-    across(two, fin, 0, late)
+    across(two, fin, 0, half)
     along(2, two, fin, 0, cut)
-    share(1, fin, 1)
+    share(1, fin, half)
     arrive(2, [*lead, 0], fin)
-    share(1, fin, 2)
+    share(1, fin, half + 1)
 
     norm1, _ = collect(1)
     ratio = norm1 / norm0
@@ -417,12 +442,15 @@
     total_fin = loop_over(REACH - 1, planes, square_fin, zero)
     for k in rest[1:]:
         arrive(2, [k], fin)
-        if REACH - 1 - k >= late:
-            share(1, fin, k + 2)
-            total_fin = square_fin(REACH - 1 - k, total_fin)
-    for d in range(late):
+        d = REACH - 1 - k
+        if k < rest[-1]:
+            share(1, fin, half + 1 + k)
+            total_fin = square_fin(d, total_fin)
+    for d in range(REACH - rest[-1]):
         total_fin = square_fin(d, total_fin)
     post(2, total_dir, total_fin)
+    for k in range(rest[-1], REACH - late):
+        share(1, fin, half + 1 + k)
     form_dir, form_fin = collect(2)
     step1 = norm1 / (form_fin + squared * form_dir)
 
@@ -461,7 +489,7 @@
     def _():
         slow_sent(0).wait_send()
 
-    fast(0).wait_send()
+    fast_sent(0)
     sol_src = spread(step0 + step1 * keep)
     sol_two = spread(step1 * step0)
 
@@ -500,8 +528,8 @@
         slow_sent(1).wait_send()
         slow_sent(2).wait_send()
 
-    fast(1).wait_send()
-    fast(2).wait_send()
+    fast_sent(1)
+    fast_sent(2)
     for r in range(3):
         exchanged(r).wait_send()
     pltpu.make_async_remote_copy(
@@ -513,10 +541,13 @@
 
 
 def write_out(sol, den, sol_hbm, den_hbm, sem):
+    planes = sol.shape[0]
+    cuts = [planes * i // 4 for i in range(5)]
     copies = [
-        pltpu.make_async_copy(sol, sol_hbm, sem.at[0]),
-        pltpu.make_async_copy(den, den_hbm, sem.at[1]),
+        pltpu.make_async_copy(sol.at[pl.ds(a, b - a)], sol_hbm.at[pl.ds(a, b - a)], sem.at[i])
+        for i, (a, b) in enumerate(zip(cuts, cuts[1:]))
     ]
+    copies.append(pltpu.make_async_copy(den, den_hbm, sem.at[4]))
     for copy in copies:
         copy.start()
     for copy in copies:
@@ -529,7 +560,7 @@
     assert planes >= 2 * REACH
     assert ny % 32 == 0 and nz % 128 == 0 and min(ny, nz) > 2 * REACH
     quarter = ny // groups
-    late = REACH // 2
+    late = REACH // 3
     early = planes - late
     f32 = jnp.float32
     field = pltpu.VMEM((planes, ny, nz), f32)
@@ -559,7 +590,7 @@
             pltpu.SMEM((1,), f32), pltpu.SMEM((1,), f32),
             pltpu.SemaphoreType.REGULAR(((n - 1).bit_length(),)),
             dma((2, planes)), dma((3,)),
-            dma((3,)), dma((3, REACH)), dma((3,)), dma((3,)), dma((3,)), dma((3,)),
+            dma((3,)), dma((3, REACH)), dma((3,)), dma((3, 2)), dma((3,)), dma((3,)),
             dma(()), dma((2, 3, 2 + REACH)), dma((3,)), dma((3,)), dma((3,)), dma((3,)),
         ],
         compiler_params=pltpu.CompilerParams(
@@ -574,7 +605,7 @@
         out_shape=(jax.ShapeDtypeStruct(sol.shape, f32), jax.ShapeDtypeStruct(den.shape, f32)),
         in_specs=[vmem] * 2,
         out_specs=(anywhere, anywhere),
-        scratch_shapes=[dma((2,))],
+        scratch_shapes=[dma((5,))],
         compiler_params=pltpu.CompilerParams(vmem_limit_bytes=2**20),
         name="write_out",
     )(sol, den)

time: 62.9 us -> 62.3 us (level)
  no operation moved by 1% of the time
where the time goes in v3:
time: 62.3 us; the launch traced here: 62.2 us
  Pallas kernels  60.2 us (97%)
  between operations  1.93 us (3%)
    pallas_call x1, Pallas kernels, body(): pl.pallas_call(functools.partial(kernel, n), out_shape=(pltpu.VMEM((plane...  58.6 us
    pallas_call x1, Pallas kernels, body(): pl.pallas_call(write_out, out_shape=(jax.ShapeDtypeStruct(sol.shape, f32)...  1.64 us

profile of v3, /device:TPU:0, one launch (start us, length us, event | category | flops | bytes accessed | tf_op | source)
XLA Modules:
  0.0 62.2 jit_solution(16177399198975687114)
XLA Ops:
  1.9 58.6 %sternheimer.1 = (f32[12,192,256]{2,1,0:T(8,128)S(1)}, f32[12,48,256]{2,1,0:T(8,128)S(1)}) custom-call(f32[12,192,256]{2,1,0:T(8,128)} %bitcast.2, f32[12,192,256]{2,1,0:T(8,128)} %pot_hbm.1, f32[12,192,256]{2,1,0:T(8,128)} %tri_hbm.1, f32[1]{0:T(128)S(6)} %copy.7.eig_hbm, f32[1]{0:T(128)S(6)} %copy.8.freq_hbm), custom_call_target="tpu_custom_call" | custom-call | tf_op jit(solution)/shard_map/sternheimer/pallas_call | solution.py:571
  60.5 1.6 %write_out.1 = (f32[12,192,256]{2,1,0:T(8,128)}, f32[12,48,256]{2,1,0:T(8,128)}) custom-call(f32[12,192,256]{2,1,0:T(8,128)S(1)} %get-tuple-element.6.sol, f32[12,48,256]{2,1,0:T(8,128)S(1)} %get-tuple-element.7.den), custom_call_target="tpu_custom_call" | custom-call | tf_op jit(solution)/shard_map/write_out/pallas_call | solution.py:603

commit v4 on v3

--- a/solution.py
+++ b/solution.py
@@ -77,6 +77,16 @@
     for slot in range(3):
         pl.semaphore_signal(barrier, inc=1, device_id={"orb": quarters[slot]})
 
+    half = REACH // 2
+    lead = [REACH - 1, REACH - 2]
+    rest = list(range(REACH - 2))
+    first_group = list(range(REACH - late))
+    arrivals = (
+        [first_group] + [[k] for k in range(REACH - late, REACH)],
+        [[*lead, 0]] + [[k] for k in rest[1:]],
+        [[*lead, 0]] + [[k] for k in rest[1:]],
+    )
+
     def at(d):
         return d + odd * (planes - 1 - 2 * d)
 
@@ -97,14 +107,26 @@
 
     rounds = met.shape[0]
 
-    def load(which, d):
-        hbm, ref = ((orb_hbm, orb), (tri_hbm, tri))[which]
-        return pltpu.make_async_copy(hbm.at[at(d)], ref.at[at(d)], ld_sem.at[which, d])
-
     order = list(range(REACH)) + list(range(planes - 1, REACH - 1, -1))
-    for d in order:
-        load(0, d).start()
-        load(1, d).start()
+    groups = [(d, 2) for d in range(0, REACH, 2)]
+    groups += [(planes - half, half), (REACH, planes - REACH - half)]
+
+    def load(i):
+        piece = span(*groups[i])
+        return [
+            pltpu.make_async_copy(hbm.at[piece], ref.at[piece], ld_sem.at[i])
+            for hbm, ref in ((orb_hbm, orb), (tri_hbm, tri))
+        ]
+
+    def loaded(d):
+        for i, (low, count) in enumerate(groups):
+            if d == (low if low < REACH else low + count - 1):
+                piece = pl.ds(0, 2 * count)
+                pltpu.make_async_copy(orb_hbm.at[piece], orb.at[piece], ld_sem.at[i]).wait()
+
+    for i in range(len(groups)):
+        for copy in load(i):
+            copy.start()
     mats = [
         pltpu.make_async_copy(pot_hbm, pot, mat_sem.at[0]),
         pltpu.make_async_copy(eig_hbm, eig, mat_sem.at[1]),
@@ -116,39 +138,38 @@
     fields = (src, img, two)
 
     def slow(r, k):
+        group = [i for i, ks in enumerate(arrivals[r]) if k in ks][0]
         return pltpu.make_async_remote_copy(
             src_ref=fields[r].at[at(k)], dst_ref=hslow.at[r, k],
-            send_sem=slow_s.at[r], recv_sem=slow_r.at[r, k],
+            send_sem=slow_s.at[min(r, 1)], recv_sem=slow_r.at[r, group],
             device_id={"grid": slow_id}, device_id_type=pl.DeviceIdType.MESH)
 
-    def slow_sent(r):
-        return pltpu.make_async_remote_copy(
-            src_ref=fields[r].at[span(0, REACH)], dst_ref=hslow.at[r],
-            send_sem=slow_s.at[r], recv_sem=slow_r.at[r, 0],
-            device_id={"grid": slow_id}, device_id_type=pl.DeviceIdType.MESH)
-
-    half = REACH // 2
+    def slow_wait(r, ks):
+        group = arrivals[r].index(ks)
+        piece = hslow.at[r, pl.ds(0, len(ks))]
+        pltpu.make_async_remote_copy(
+            src_ref=piece, dst_ref=piece,
+            send_sem=slow_s.at[min(r, 1)], recv_sem=slow_r.at[r, group],
+            device_id={"grid": slow_id}, device_id_type=pl.DeviceIdType.MESH).wait_recv()
+
+    def sent(low, count, buffer, sem):
+        piece = buffer.at[pl.ds(low, count)]
+        pltpu.make_async_remote_copy(
+            src_ref=piece, dst_ref=piece, send_sem=sem, recv_sem=slow_r.at[0, 0],
+            device_id={"grid": fast_id}, device_id_type=pl.DeviceIdType.MESH).wait_send()
 
     def fast(r, i):
         return pltpu.make_async_remote_copy(
             src_ref=fields[r].at[span(planes - half * (i + 1), half)],
             dst_ref=hfast.at[r, pl.ds(half * (1 - i) + odd * half * (2 * i - 1), half)],
-            send_sem=fast_s.at[r], recv_sem=fast_r.at[r, i],
+            send_sem=fast_s.at[min(r, 1)], recv_sem=fast_r.at[i],
             device_id={"grid": fast_id}, device_id_type=pl.DeviceIdType.MESH)
 
-    def fast_send(r):
-        fast(r, 0).start()
-        fast(r, 1).start()
-
-    def fast_wait(r):
-        fast(r, 0).wait_recv()
-        fast(r, 1).wait_recv()
-
-    def fast_sent(r):
-        pltpu.make_async_remote_copy(
+    def fast_both(r):
+        return pltpu.make_async_remote_copy(
             src_ref=fields[r].at[span(planes - REACH, REACH)], dst_ref=hfast.at[r],
-            send_sem=fast_s.at[r], recv_sem=fast_r.at[r, 0],
-            device_id={"grid": fast_id}, device_id_type=pl.DeviceIdType.MESH).wait_send()
+            send_sem=fast_s.at[1], recv_sem=fast_r.at[1 + r],
+            device_id={"grid": fast_id}, device_id_type=pl.DeviceIdType.MESH)
 
     def send(r, *ks):
         @pl.when(has_slow)
@@ -169,14 +190,19 @@
         piece = pl.ds(d - late, count)
         return pltpu.make_async_remote_copy(
             src_ref=ship.at[field, slot, piece], dst_ref=land.at[field, slot, piece],
-            send_sem=ship_s, recv_sem=ship_r.at[field, slot, sem],
+            send_sem=ship_s, recv_sem=ship_r.at[field, sem],
             device_id={"orb": quarters[slot]}, device_id_type=pl.DeviceIdType.MESH)
 
+    def ship_wait(field, d, count, sem):
+        piece = pl.ds(d - late, count)
+        pltpu.make_async_remote_copy(
+            src_ref=ship.at[field, pl.ds(0, 3), piece], dst_ref=land.at[field, pl.ds(0, 3), piece],
+            send_sem=ship_s, recv_sem=ship_r.at[field, sem],
+            device_id={"orb": both}, device_id_type=pl.DeviceIdType.MESH).wait_recv()
+
     cut = 2 * REACH - half
-    lead = [REACH - 1, REACH - 2]
-    rest = list(range(REACH - 2))
     batches = (
-        ((REACH, planes - REACH), (late, REACH - late)),
+        ((REACH, half), (REACH + half, planes - REACH - half), (late, REACH - late)),
         ((2 * REACH - 1, planes - 2 * REACH + 1),)
         + tuple((d, 1) for d in range(2 * REACH - 2, cut - 1, -1))
         + ((REACH, cut - REACH),)
@@ -196,8 +222,7 @@
     def arrive(r, ks, acc):
         @pl.when(has_slow)
         def _():
-            for k in ks:
-                slow(r, k).wait_recv()
+            slow_wait(r, ks)
 
             def step(s, carry):
                 rows = rows_of(s, wide)
@@ -279,13 +304,13 @@
     def exchange(r, j, slot):
         return pltpu.make_async_remote_copy(
             src_ref=sums.at[r, slot], dst_ref=sums.at[r, slot],
-            send_sem=sum_s.at[r], recv_sem=sum_r.at[r],
+            send_sem=sum_s, recv_sem=sum_r.at[r],
             device_id={"grid": lax.rem(g + j, n)}, device_id_type=pl.DeviceIdType.MESH)
 
     def exchanged(r):
         return pltpu.make_async_remote_copy(
             src_ref=sums.at[r, pl.ds(0, n - 1)], dst_ref=sums.at[r, pl.ds(0, n - 1)],
-            send_sem=sum_s.at[r], recv_sem=sum_r.at[r],
+            send_sem=sum_s, recv_sem=sum_r.at[r],
             device_id={"grid": fast_id}, device_id_type=pl.DeviceIdType.MESH)
 
     def post(r, *totals):
@@ -310,8 +335,7 @@
 
     total_src = zero
     for d in order:
-        load(0, d).wait()
-        load(1, d).wait()
+        loaded(d)
 
         def step(s, carry, d=d):
             rows = rows_of(s, wide)
@@ -334,14 +358,18 @@
     energy = eig[0]
     squared = freq[0] * freq[0]
 
-    across(src, img, REACH, planes)
+    across(src, img, REACH, REACH + half)
+    fast(0, 0).wait_recv()
+    along(0, src, img, REACH, REACH + half)
+    share(0, img, 0)
+    across(src, img, REACH + half, planes)
     if rounds > 1:
         met_by(0)
         meet(1)
-    fast_wait(0)
-    along(0, src, img, REACH, planes)
-    fast_send(1)
-    share(0, img, 0)
+    fast(0, 1).wait_recv()
+    along(0, src, img, REACH + half, planes)
+    fast_both(1).start()
+    share(0, img, 1)
     across(src, img, 0, REACH)
     along(0, src, img, 0, REACH)
     for i in range(1, rounds - 1):
@@ -353,7 +381,7 @@
     early = list(range(REACH - late))
     arrive(0, early, img)
     send(1, *lead)
-    share(0, img, 1)
+    share(0, img, 2)
     for k in early:
         total_img = square_of(img, REACH - 1 - k, total_img)
     across(img, two, late, planes)
@@ -366,12 +394,12 @@
     post(0, total_src, total_img)
     send(1, *rest)
     across(img, two, 0, 1)
-    fast_wait(1)
+    fast_both(1).wait_recv()
     along(1, img, two, 0, planes)
-    fast_send(2)
+    fast_both(2).start()
 
     across(two, fin, REACH, planes)
-    fast_wait(2)
+    fast_both(2).wait_recv()
     arrive(1, [*lead, 0], two)
     send(2, REACH - 1)
     across(two, fin, REACH - 1, REACH)
@@ -462,7 +490,7 @@
     def tell(slot):
         return pltpu.make_async_remote_copy(
             src_ref=mix.at[3], dst_ref=mix.at[slot],
-            send_sem=mix_s.at[slot], recv_sem=mix_r.at[slot],
+            send_sem=mix_s, recv_sem=mix_r,
             device_id={"orb": quarters[slot]}, device_id_type=pl.DeviceIdType.MESH)
 
     near_img_row = spread(near_img)
@@ -473,10 +501,18 @@
         return orb[at(d), rows, :] * (
             near_img_row * img[at(d), rows, :] + near_fin_row * fin[at(d), rows, :])
 
+    def all_of(source, target, send, recv):
+        return pltpu.make_async_remote_copy(
+            src_ref=source, dst_ref=target, send_sem=send, recv_sem=recv,
+            device_id={"orb": both}, device_id_type=pl.DeviceIdType.MESH)
+
+    told = all_of(mix.at[pl.ds(0, 3)], mix.at[pl.ds(0, 3)], mix_s, mix_r)
+    late_all = all_of(ship_late, land_late, late_s, late_r)
+
     def late_copy(slot):
         return pltpu.make_async_remote_copy(
             src_ref=ship_late.at[slot], dst_ref=land_late.at[slot],
-            send_sem=late_s.at[slot], recv_sem=late_r.at[slot],
+            send_sem=late_s, recv_sem=late_r,
             device_id={"orb": quarters[slot]}, device_id_type=pl.DeviceIdType.MESH)
 
     for slot in range(3):
@@ -487,9 +523,9 @@
 
     @pl.when(has_slow)
     def _():
-        slow_sent(0).wait_send()
-
-    fast_sent(0)
+        sent(0, 1, hslow, slow_s.at[0])
+
+    sent(0, 1, hfast, fast_s.at[0])
     sol_src = spread(step0 + step1 * keep)
     sol_two = spread(step1 * step0)
 
@@ -504,40 +540,32 @@
     lax.fori_loop(0, planes, solve, 0)
     for d in range(planes):
         dens[at(d)] = respond(3, d)
-    for slot in range(3):
-        tell(slot).wait_recv()
+    told.wait_recv()
     for batch, (d, count) in enumerate(batches[0]):
-        for slot in range(3):
-            ship_copy(0, slot, d, count, batch).wait_recv()
+        ship_wait(0, d, count, batch)
     for batch, (d, count) in enumerate(batches[1]):
-        for slot in range(3):
-            ship_copy(1, slot, d, count, batch).wait_recv()
+        ship_wait(1, d, count, batch)
         for e in range(d, d + count):
             total = dens[at(e)]
             for slot in range(3):
                 for field in range(2):
                     total = total + mix[slot, field, 0:1, :] * land[field, slot, e - late]
             dens[at(e)] = total
-    for slot in range(3):
-        late_copy(slot).wait_recv()
+    late_all.wait_recv()
     for d in range(late):
         dens[at(d)] = dens[at(d)] + (land_late[0, d] + land_late[1, d] + land_late[2, d])
 
     @pl.when(has_slow)
     def _():
-        slow_sent(1).wait_send()
-        slow_sent(2).wait_send()
-
-    fast_sent(1)
-    fast_sent(2)
-    for r in range(3):
-        exchanged(r).wait_send()
-    pltpu.make_async_remote_copy(
-        src_ref=ship, dst_ref=land, send_sem=ship_s, recv_sem=ship_r.at[0, 0, 0],
-        device_id={"orb": both}, device_id_type=pl.DeviceIdType.MESH).wait_send()
-    for slot in range(3):
-        tell(slot).wait_send()
-        late_copy(slot).wait_send()
+        sent(1, 2, hslow, slow_s.at[1])
+
+    sent(1, 2, hfast, fast_s.at[1])
+    all_of(
+        sums.at[pl.ds(0, 3), pl.ds(0, n - 1)], sums.at[pl.ds(0, 3), pl.ds(0, n - 1)],
+        sum_s, sum_r.at[0]).wait_send()
+    all_of(ship, land, ship_s, ship_r.at[0, 0]).wait_send()
+    told.wait_send()
+    late_all.wait_send()
 
 
 def write_out(sol, den, sol_hbm, den_hbm, sem):
@@ -589,9 +617,9 @@
             pltpu.VMEM((4, 2, 8, nz), f32),
             pltpu.SMEM((1,), f32), pltpu.SMEM((1,), f32),
             pltpu.SemaphoreType.REGULAR(((n - 1).bit_length(),)),
-            dma((2, planes)), dma((3,)),
-            dma((3,)), dma((3, REACH)), dma((3,)), dma((3, 2)), dma((3,)), dma((3,)),
-            dma(()), dma((2, 3, 2 + REACH)), dma((3,)), dma((3,)), dma((3,)), dma((3,)),
+            dma((2 + REACH // 2,)), dma((3,)),
+            dma((2,)), dma((3, max(1 + late, REACH - 2))), dma((2,)), dma((4,)), dma(()), dma((3,)),
+            dma(()), dma((2, 2 + REACH)), dma(()), dma(()), dma(()), dma(()),
         ],
         compiler_params=pltpu.CompilerParams(
             collective_id=0, has_side_effects=True, vmem_limit_bytes=50 * 2**20),

time: 62.3 us -> 60.2 us (0.966)
  Pallas kernels: 60.2 us -> 58.2 us
    pallas_call x1, Pallas kernels: 58.6 us -> 56.5 us  [body(): pl.pallas_call(functools.partial(kernel, n), out_shape=(pltpu.VMEM((plane...]
where the time goes in v4:
time: 60.2 us; the launch traced here: 60.1 us
  Pallas kernels  58.2 us (97%)
  between operations  1.93 us (3%)
    pallas_call x1, Pallas kernels, body(): pl.pallas_call(functools.partial(kernel, n), out_shape=(pltpu.VMEM((plane...  56.5 us
    pallas_call x1, Pallas kernels, body(): pl.pallas_call(write_out, out_shape=(jax.ShapeDtypeStruct(sol.shape, f32)...  1.64 us

profile of v4, /device:TPU:0, one launch (start us, length us, event | category | flops | bytes accessed | tf_op | source)
XLA Modules:
  0.0 60.1 jit_solution(8860836683898216372)
XLA Ops:
  1.9 56.5 %sternheimer.1 = (f32[12,192,256]{2,1,0:T(8,128)S(1)}, f32[12,48,256]{2,1,0:T(8,128)S(1)}) custom-call(f32[12,192,256]{2,1,0:T(8,128)} %bitcast.2, f32[12,192,256]{2,1,0:T(8,128)} %pot_hbm.1, f32[12,192,256]{2,1,0:T(8,128)} %tri_hbm.1, f32[1]{0:T(128)S(6)} %copy.7.eig_hbm, f32[1]{0:T(128)S(6)} %copy.8.freq_hbm), custom_call_target="tpu_custom_call" | custom-call | tf_op jit(solution)/shard_map/sternheimer/pallas_call | solution.py:599
  58.4 1.6 %write_out.1 = (f32[12,192,256]{2,1,0:T(8,128)}, f32[12,48,256]{2,1,0:T(8,128)}) custom-call(f32[12,192,256]{2,1,0:T(8,128)S(1)} %get-tuple-element.6.sol, f32[12,48,256]{2,1,0:T(8,128)S(1)} %get-tuple-element.7.den), custom_call_target="tpu_custom_call" | custom-call | tf_op jit(solution)/shard_map/write_out/pallas_call | solution.py:631

commit v5 on v4

--- a/solution.py
+++ b/solution.py
@@ -74,7 +74,7 @@
         pl.semaphore_signal(barrier, inc=1, device_id={"grid": slow_id})
 
     pl.semaphore_signal(barrier, inc=1, device_id={"grid": fast_id})
-    for slot in range(3):
+    for slot in (1, 2):
         pl.semaphore_signal(barrier, inc=1, device_id={"orb": quarters[slot]})
 
     half = REACH // 2
@@ -87,6 +87,8 @@
         [[*lead, 0]] + [[k] for k in rest[1:]],
     )
 
+    before = [sum(len(group) for group in arrivals[:r]) for r in range(3)]
+
     def at(d):
         return d + odd * (planes - 1 - 2 * d)
 
@@ -105,7 +107,7 @@
         pl.semaphore_wait(
             met.at[i], jnp.where(g >= reach, 1, 0) + jnp.where(g + reach < n, 1, 0))
 
-    rounds = met.shape[0]
+    rounds = met.shape[0] - 1
 
     order = list(range(REACH)) + list(range(planes - 1, REACH - 1, -1))
     groups = [(d, 2) for d in range(0, REACH, 2)]
@@ -141,7 +143,7 @@
         group = [i for i, ks in enumerate(arrivals[r]) if k in ks][0]
         return pltpu.make_async_remote_copy(
             src_ref=fields[r].at[at(k)], dst_ref=hslow.at[r, k],
-            send_sem=slow_s.at[min(r, 1)], recv_sem=slow_r.at[r, group],
+            send_sem=slow_s.at[min(r, 1)], recv_sem=slow_r.at[before[r] + group],
             device_id={"grid": slow_id}, device_id_type=pl.DeviceIdType.MESH)
 
     def slow_wait(r, ks):
@@ -149,13 +151,13 @@
         piece = hslow.at[r, pl.ds(0, len(ks))]
         pltpu.make_async_remote_copy(
             src_ref=piece, dst_ref=piece,
-            send_sem=slow_s.at[min(r, 1)], recv_sem=slow_r.at[r, group],
+            send_sem=slow_s.at[min(r, 1)], recv_sem=slow_r.at[before[r] + group],
             device_id={"grid": slow_id}, device_id_type=pl.DeviceIdType.MESH).wait_recv()
 
     def sent(low, count, buffer, sem):
         piece = buffer.at[pl.ds(low, count)]
         pltpu.make_async_remote_copy(
-            src_ref=piece, dst_ref=piece, send_sem=sem, recv_sem=slow_r.at[0, 0],
+            src_ref=piece, dst_ref=piece, send_sem=sem, recv_sem=slow_r.at[0],
             device_id={"grid": fast_id}, device_id_type=pl.DeviceIdType.MESH).wait_send()
 
     def fast(r, i):
@@ -186,23 +188,25 @@
     def over(step, init, count=wide):
         return lax.fori_loop(0, ny // count, step, init)
 
-    def ship_copy(field, slot, d, count, sem):
+    def ship_copy(field, slot, d, count):
         piece = pl.ds(d - late, count)
         return pltpu.make_async_remote_copy(
             src_ref=ship.at[field, slot, piece], dst_ref=land.at[field, slot, piece],
-            send_sem=ship_s, recv_sem=ship_r.at[field, sem],
+            send_sem=ship_s, recv_sem=ship_r.at[field],
             device_id={"orb": quarters[slot]}, device_id_type=pl.DeviceIdType.MESH)
 
-    def ship_wait(field, d, count, sem):
-        piece = pl.ds(d - late, count)
+    def ship_wait(field):
         pltpu.make_async_remote_copy(
-            src_ref=ship.at[field, pl.ds(0, 3), piece], dst_ref=land.at[field, pl.ds(0, 3), piece],
-            send_sem=ship_s, recv_sem=ship_r.at[field, sem],
+            src_ref=ship.at[field], dst_ref=land.at[field],
+            send_sem=ship_s, recv_sem=ship_r.at[field],
             device_id={"orb": both}, device_id_type=pl.DeviceIdType.MESH).wait_recv()
 
     cut = 2 * REACH - half
     batches = (
-        ((REACH, half), (REACH + half, planes - REACH - half), (late, REACH - late)),
+        (
+            (REACH, 1), (REACH + 1, half - 1), (REACH + half, planes - REACH - half),
+            (late, REACH - late),
+        ),
         ((2 * REACH - 1, planes - 2 * REACH + 1),)
         + tuple((d, 1) for d in range(2 * REACH - 2, cut - 1, -1))
         + ((REACH, cut - REACH),)
@@ -215,7 +219,7 @@
             rows = rows_in(slot)
             for e in range(d, d + count):
                 ship[field, slot, e - late] = orb[at(e), rows, :] * value[at(e), rows, :]
-            ship_copy(field, slot, d, count, batch).start()
+            ship_copy(field, slot, d, count).start()
 
     zero = jnp.zeros((wide, nz), jnp.float32)
 
@@ -345,7 +349,8 @@
 
         total_src = over(step, total_src)
         if d == order[0]:
-            pl.semaphore_wait(barrier, 4 + has_slow.astype(jnp.int32))
+            pl.semaphore_wait(barrier, 3 + has_slow.astype(jnp.int32))
+            pl.semaphore_signal(met.at[rounds], inc=1, device_id={"orb": first})
             meet(0)
         if d < REACH:
             send(0, d)
@@ -358,10 +363,14 @@
     energy = eig[0]
     squared = freq[0] * freq[0]
 
-    across(src, img, REACH, REACH + half)
+    across(src, img, REACH, REACH + 1)
     fast(0, 0).wait_recv()
-    along(0, src, img, REACH, REACH + half)
+    along(0, src, img, REACH, REACH + 1)
+    pl.semaphore_wait(met.at[rounds], 1)
     share(0, img, 0)
+    across(src, img, REACH + 1, REACH + half)
+    along(0, src, img, REACH + 1, REACH + half)
+    share(0, img, 1)
     across(src, img, REACH + half, planes)
     if rounds > 1:
         met_by(0)
@@ -369,7 +378,7 @@
     fast(0, 1).wait_recv()
     along(0, src, img, REACH + half, planes)
     fast_both(1).start()
-    share(0, img, 1)
+    share(0, img, 2)
     across(src, img, 0, REACH)
     along(0, src, img, 0, REACH)
     for i in range(1, rounds - 1):
@@ -381,7 +390,7 @@
     early = list(range(REACH - late))
     arrive(0, early, img)
     send(1, *lead)
-    share(0, img, 2)
+    share(0, img, 3)
     for k in early:
         total_img = square_of(img, REACH - 1 - k, total_img)
     across(img, two, late, planes)
@@ -541,16 +550,14 @@
     for d in range(planes):
         dens[at(d)] = respond(3, d)
     told.wait_recv()
-    for batch, (d, count) in enumerate(batches[0]):
-        ship_wait(0, d, count, batch)
-    for batch, (d, count) in enumerate(batches[1]):
-        ship_wait(1, d, count, batch)
-        for e in range(d, d + count):
-            total = dens[at(e)]
-            for slot in range(3):
-                for field in range(2):
-                    total = total + mix[slot, field, 0:1, :] * land[field, slot, e - late]
-            dens[at(e)] = total
+    for field in range(2):
+        ship_wait(field)
+    for e in range(late, planes):
+        total = dens[at(e)]
+        for slot in range(3):
+            for field in range(2):
+                total = total + mix[slot, field, 0:1, :] * land[field, slot, e - late]
+        dens[at(e)] = total
     late_all.wait_recv()
     for d in range(late):
         dens[at(d)] = dens[at(d)] + (land_late[0, d] + land_late[1, d] + land_late[2, d])
@@ -563,7 +570,7 @@
     all_of(
         sums.at[pl.ds(0, 3), pl.ds(0, n - 1)], sums.at[pl.ds(0, 3), pl.ds(0, n - 1)],
         sum_s, sum_r.at[0]).wait_send()
-    all_of(ship, land, ship_s, ship_r.at[0, 0]).wait_send()
+    all_of(ship, land, ship_s, ship_r.at[0]).wait_send()
     told.wait_send()
     late_all.wait_send()
 
@@ -616,10 +623,10 @@
             pltpu.VMEM((3, late, quarter, nz), f32),
             pltpu.VMEM((4, 2, 8, nz), f32),
             pltpu.SMEM((1,), f32), pltpu.SMEM((1,), f32),
-            pltpu.SemaphoreType.REGULAR(((n - 1).bit_length(),)),
+            pltpu.SemaphoreType.REGULAR(((n - 1).bit_length() + 1,)),
             dma((2 + REACH // 2,)), dma((3,)),
-            dma((2,)), dma((3, max(1 + late, REACH - 2))), dma((2,)), dma((4,)), dma(()), dma((3,)),
-            dma(()), dma((2, 2 + REACH)), dma(()), dma(()), dma(()), dma(()),
+            dma((2,)), dma((1 + late + 2 * (REACH - 2),)), dma((2,)), dma((4,)), dma(()), dma((3,)),
+            dma(()), dma((2,)), dma(()), dma(()), dma(()), dma(()),
         ],
         compiler_params=pltpu.CompilerParams(
             collective_id=0, has_side_effects=True, vmem_limit_bytes=50 * 2**20),

time: 60.2 us -> 60 us (level)
  no operation moved by 1% of the time
where the time goes in v5:
time: 60 us; the launch traced here: 59.9 us
  Pallas kernels  58 us (97%)
  between operations  1.93 us (3%)
    pallas_call x1, Pallas kernels, body(): pl.pallas_call(functools.partial(kernel, n), out_shape=(pltpu.VMEM((plane...  56.3 us
    pallas_call x1, Pallas kernels, body(): pl.pallas_call(write_out, out_shape=(jax.ShapeDtypeStruct(sol.shape, f32)...  1.64 us

profile of v5, /device:TPU:0, one launch (start us, length us, event | category | flops | bytes accessed | tf_op | source)
XLA Modules:
  0.0 59.9 jit_solution(17802669872867914121)
XLA Ops:
  1.9 56.3 %sternheimer.1 = (f32[12,192,256]{2,1,0:T(8,128)S(1)}, f32[12,48,256]{2,1,0:T(8,128)S(1)}) custom-call(f32[12,192,256]{2,1,0:T(8,128)} %bitcast.2, f32[12,192,256]{2,1,0:T(8,128)} %pot_hbm.1, f32[12,192,256]{2,1,0:T(8,128)} %tri_hbm.1, f32[1]{0:T(128)S(6)} %copy.7.eig_hbm, f32[1]{0:T(128)S(6)} %copy.8.freq_hbm), custom_call_target="tpu_custom_call" | custom-call | tf_op jit(solution)/shard_map/sternheimer/pallas_call | solution.py:606
  58.2 1.6 %write_out.1 = (f32[12,192,256]{2,1,0:T(8,128)}, f32[12,48,256]{2,1,0:T(8,128)}) custom-call(f32[12,192,256]{2,1,0:T(8,128)S(1)} %get-tuple-element.6.sol, f32[12,48,256]{2,1,0:T(8,128)S(1)} %get-tuple-element.7.den), custom_call_target="tpu_custom_call" | custom-call | tf_op jit(solution)/shard_map/write_out/pallas_call | solution.py:638

commit v6 on v5

--- a/solution.py
+++ b/solution.py
@@ -493,8 +493,8 @@
 
     near_img = -4.0 * (step0 + step1 * keep)
     near_fin = 4.0 * (step1 * step0)
-    mix[3, 0] = jnp.broadcast_to(near_img, mix.shape[2:])
-    mix[3, 1] = jnp.broadcast_to(near_fin, mix.shape[2:])
+    mix[3, 0:1, :] = spread(near_img)
+    mix[3, 1:2, :] = spread(near_fin)
 
     def tell(slot):
         return pltpu.make_async_remote_copy(
@@ -556,7 +556,7 @@
         total = dens[at(e)]
         for slot in range(3):
             for field in range(2):
-                total = total + mix[slot, field, 0:1, :] * land[field, slot, e - late]
+                total = total + mix[slot, field:field + 1, :] * land[field, slot, e - late]
         dens[at(e)] = total
     late_all.wait_recv()
     for d in range(late):
@@ -621,7 +621,7 @@
             pltpu.VMEM((2, 3, early, quarter, nz), f32),
             pltpu.VMEM((3, late, quarter, nz), f32),
             pltpu.VMEM((3, late, quarter, nz), f32),
-            pltpu.VMEM((4, 2, 8, nz), f32),
+            pltpu.VMEM((4, 2, nz), f32),
             pltpu.SMEM((1,), f32), pltpu.SMEM((1,), f32),
             pltpu.SemaphoreType.REGULAR(((n - 1).bit_length() + 1,)),
             dma((2 + REACH // 2,)), dma((3,)),

time: 60 us -> 59.4 us (0.990)
  Pallas kernels: 58 us -> 57.3 us
    pallas_call x1, Pallas kernels: 56.3 us -> 55.7 us  [body(): pl.pallas_call(functools.partial(kernel, n), out_shape=(pltpu.VMEM((plane...]
where the time goes in v6:
time: 59.4 us; the launch traced here: 59.3 us
  Pallas kernels  57.3 us (96%)
  between operations  1.93 us (3%)
    pallas_call x1, Pallas kernels, body(): pl.pallas_call(functools.partial(kernel, n), out_shape=(pltpu.VMEM((plane...  55.7 us
    pallas_call x1, Pallas kernels, body(): pl.pallas_call(write_out, out_shape=(jax.ShapeDtypeStruct(sol.shape, f32)...  1.64 us

profile of v6, /device:TPU:0, one launch (start us, length us, event | category | flops | bytes accessed | tf_op | source)
XLA Modules:
  0.0 59.3 jit_solution(1507925257156359583)
XLA Ops:
  1.9 55.7 %sternheimer.1 = (f32[12,192,256]{2,1,0:T(8,128)S(1)}, f32[12,48,256]{2,1,0:T(8,128)S(1)}) custom-call(f32[12,192,256]{2,1,0:T(8,128)} %bitcast.2, f32[12,192,256]{2,1,0:T(8,128)} %pot_hbm.1, f32[12,192,256]{2,1,0:T(8,128)} %tri_hbm.1, f32[1]{0:T(128)S(6)} %copy.7.eig_hbm, f32[1]{0:T(128)S(6)} %copy.8.freq_hbm), custom_call_target="tpu_custom_call" | custom-call | tf_op jit(solution)/shard_map/sternheimer/pallas_call | solution.py:606
  57.6 1.6 %write_out.1 = (f32[12,192,256]{2,1,0:T(8,128)}, f32[12,48,256]{2,1,0:T(8,128)}) custom-call(f32[12,192,256]{2,1,0:T(8,128)S(1)} %get-tuple-element.6.sol, f32[12,48,256]{2,1,0:T(8,128)S(1)} %get-tuple-element.7.den), custom_call_target="tpu_custom_call" | custom-call | tf_op jit(solution)/shard_map/write_out/pallas_call | solution.py:638
